TPU v7x, 32 devices: a whole 2x2x4 slice. The times are simulated.
32 devices in a mesh: fsdp: 8 (over y, x, core), tensor: 4 (over z).
Axes of the slice: x: 2, y: 2, z: 4, core: 2. Of those that a mesh axis runs over, the one named last changes fastest.
Arguments:
- inputs: bfloat16 [32, 577, 1024], P('fsdp'), may hold values from -6 to 6
- lengths: int32 [32], P('fsdp'), may hold values from 144 to 577, as said below
- norm_gains: bfloat16 [2, 1024], P(None, 'fsdp'), may hold values from 0.5 to 1.5
- norm_shifts: bfloat16 [2, 1024], P(None, 'fsdp'), may hold values from -1.5 to 1.5
- w_qkv: bfloat16 [3, 1024, 1024], P(None, 'fsdp', 'tensor'), may hold values from -0.1875 to 0.1875
- bias_qv: bfloat16 [2, 1024], P(None, 'tensor'), may hold values from -3 to 3
- w_out: bfloat16 [1024, 1024], P('tensor', 'fsdp'), may hold values from -1.5 to 1.5
- out_bias: bfloat16 [2, 1024], P(None, 'fsdp'), may hold values from -1.5 to 1.5
- w_up: bfloat16 [1024, 4096], P('fsdp', 'tensor'), may hold values from -0.1875 to 0.1875
- b_up: bfloat16 [4096], P('tensor'), may hold values from -3 to 3
- w_down: bfloat16 [4096, 1024], P('tensor', 'fsdp'), may hold values from -0.375 to 0.375
- cotangent: bfloat16 [32, 577, 1024], P('fsdp'), may hold values from -6 to 6
Outputs:
- output: bfloat16 [32, 577, 1024], P('fsdp')
- grad_input: float32 [32, 577, 1024], P('fsdp')
- grad_gains: float32 [2, 1024], P(None, 'fsdp')
- grad_shifts: float32 [2, 1024], P(None, 'fsdp')
- grad_qkv: float32 [3, 1024, 1024], P(None, 'fsdp', 'tensor')
- grad_bias_qv: float32 [2, 1024], P(None, 'tensor')
- grad_out: float32 [1024, 1024], P('tensor', 'fsdp')
- grad_out_bias: float32 [2, 1024], P(None, 'fsdp')
- grad_up: float32 [1024, 4096], P('fsdp', 'tensor')
- grad_b_up: float32 [4096], P('tensor')
- grad_down: float32 [4096, 1024], P('tensor', 'fsdp')
Inputs may be any that keep to these rules, and one draw needn't show every extreme that they name: lengths[b] counts the valid leading tokens of image b; some image has all 577 valid and some has 144.
All inputs are finite; a program needn't handle non-finite values.
Results may differ from a plain program's by a relative error of at most 0.02.
Values may be sent and summed in bfloat16 or wider, within the bound.
A program may use at most 256 MiB of HBM per device.

v0:
```python
import jax
import jax.numpy as jnp
from jax import lax
from jax.sharding import PartitionSpec as P

HEAD = 64
epsilon = 1e-06
half_root = 0.7071067811865476
density_scale = 0.3989422804014327


def normalize(tokens):
    average = jnp.mean(tokens, axis=-1, keepdims=True)
    centred = tokens - average
    spread = jnp.mean(centred * centred, axis=-1, keepdims=True)
    inverse = lax.rsqrt(spread + epsilon)
    return (centred * inverse, inverse)


def normalize_back(incoming, normed, inverse, gain):
    scaled = incoming * gain
    return inverse * (
        scaled
        - jnp.mean(scaled, axis=-1, keepdims=True)
        - normed * jnp.mean(scaled * normed, axis=-1, keepdims=True)
    )


def masked_scores(query_heads, key_heads, valid, scale):
    scores = (
        jnp.einsum("bqhe,bkhe->bhqk", query_heads, key_heads, preferred_element_type=jnp.float32)
        * scale
    )
    return jnp.where(valid[:, None, None, :], scores, -jnp.inf)


def local(
    inputs,
    lengths,
    norm_gains,
    norm_shifts,
    w_qkv,
    bias_qv,
    w_out,
    out_bias,
    w_up,
    b_up,
    w_down,
    cotangent,
):
    batch, seq_len, width = inputs.shape
    tokens = batch * seq_len
    local_width = w_qkv.shape[2]
    local_heads = local_width // HEAD
    scale = HEAD ** (-0.5)
    gathered = (
        lax.all_gather(w_qkv, "fsdp", axis=1, tiled=True),
        lax.all_gather(w_out, "fsdp", axis=1, tiled=True),
        lax.all_gather(w_up, "fsdp", axis=0, tiled=True),
        lax.all_gather(w_down, "fsdp", axis=1, tiled=True),
        lax.all_gather(norm_gains, "fsdp", axis=1, tiled=True),
        lax.all_gather(norm_shifts, "fsdp", axis=1, tiled=True),
        lax.all_gather(out_bias, "fsdp", axis=1, tiled=True),
    )
    full_qkv, full_out, full_up, full_down, all_gains, all_shifts, all_bias = gathered
    gain_rows = all_gains.astype(jnp.float32)
    shift_rows = all_shifts.astype(jnp.float32)
    bias_rows = all_bias.astype(jnp.float32)
    proj_bias = bias_qv.astype(jnp.float32)
    hidden_bias = b_up.astype(jnp.float32)
    flat_in = inputs.reshape(tokens, width).astype(jnp.float32)
    normed_one, inverse_one = normalize(flat_in)
    hidden_one = (normed_one * gain_rows[0] + shift_rows[0]).astype(jnp.bfloat16)
    projected = jnp.einsum("rd,cde->cre", hidden_one, full_qkv, preferred_element_type=jnp.float32)
    queries = (projected[0] + proj_bias[0]).astype(jnp.bfloat16)
    key_rows = projected[1].astype(jnp.bfloat16)
    value_rows = (projected[2] + proj_bias[1]).astype(jnp.bfloat16)
    head_shape = (batch, seq_len, local_heads, HEAD)
    query_heads = queries.reshape(head_shape)
    key_heads = key_rows.reshape(head_shape)
    value_heads = value_rows.reshape(head_shape)
    valid = lax.broadcasted_iota(jnp.int32, (batch, seq_len), 1) < lengths[:, None]
    scores = masked_scores(query_heads, key_heads, valid, scale)
    top = jnp.max(scores, axis=-1, keepdims=True)
    log_total = top + jnp.log(jnp.sum(jnp.exp(scores - top), axis=-1, keepdims=True))
    weights_b = jnp.exp(scores - log_total).astype(jnp.bfloat16)
    attended_heads = jnp.einsum(
        "bhqk,bkhe->bqhe", weights_b, value_heads, preferred_element_type=jnp.float32
    ).astype(jnp.bfloat16)
    attended = attended_heads.reshape(tokens, local_width)
    attn_total = lax.psum(
        jnp.dot(attended, full_out, preferred_element_type=jnp.float32).astype(jnp.bfloat16),
        "tensor",
    ).astype(jnp.float32)
    middle = flat_in + (attn_total + bias_rows[0])
    normed_two, inverse_two = normalize(middle)
    hidden_two = (normed_two * gain_rows[1] + shift_rows[1]).astype(jnp.bfloat16)
    before = jnp.dot(hidden_two, full_up, preferred_element_type=jnp.float32) + hidden_bias
    activated = jax.nn.gelu(before, approximate=False).astype(jnp.bfloat16)
    mlp_total = lax.psum(
        jnp.dot(activated, full_down, preferred_element_type=jnp.float32).astype(jnp.bfloat16),
        "tensor",
    ).astype(jnp.float32)
    result = (middle + (mlp_total + bias_rows[1])).astype(jnp.bfloat16)
    back_qkv, back_out, back_up, back_down = (full_qkv, full_out, full_up, full_down)
    grad_rows = cotangent.reshape(tokens, width)
    grad_f = grad_rows.astype(jnp.float32)
    grad_down = jnp.einsum("rf,rd->fd", activated, grad_rows, preferred_element_type=jnp.float32)
    dact = jnp.einsum("rd,fd->rf", grad_rows, back_down, preferred_element_type=jnp.float32)
    normal_cdf = 0.5 * (1.0 + jax.scipy.special.erf(before * half_root))
    density = jnp.exp(-0.5 * before * before) * density_scale
    dbefore = dact * (normal_cdf + before * density)
    dbefore_b = dbefore.astype(jnp.bfloat16)
    grad_b_up = jnp.sum(dbefore, axis=0)
    grad_up = jnp.einsum("rd,rf->df", hidden_two, dbefore_b, preferred_element_type=jnp.float32)
    dhidden_two = lax.psum(
        jnp.einsum("rf,df->rd", dbefore_b, back_up, preferred_element_type=jnp.float32).astype(
            jnp.bfloat16
        ),
        "tensor",
    ).astype(jnp.float32)
    dmiddle = grad_f + normalize_back(dhidden_two, normed_two, inverse_two, gain_rows[1])
    dmiddle_b = dmiddle.astype(jnp.bfloat16)
    grad_out = jnp.einsum("rk,rd->kd", attended, dmiddle_b, preferred_element_type=jnp.float32)
    grad_out_bias = jnp.stack([jnp.sum(dmiddle, axis=0), jnp.sum(grad_f, axis=0)])
    dattended = jnp.einsum(
        "rd,kd->rk", dmiddle_b, back_out, preferred_element_type=jnp.float32
    ).astype(jnp.bfloat16)
    dattended_heads = dattended.reshape(head_shape)
    again_scores = masked_scores(query_heads, key_heads, valid, scale)
    prob = jnp.exp(again_scores - log_total)
    again_weights = prob.astype(jnp.bfloat16)
    dprob = jnp.einsum(
        "bqhe,bkhe->bhqk", dattended_heads, value_heads, preferred_element_type=jnp.float32
    )
    delta = jnp.einsum(
        "bqhe,bqhe->bhq", dattended_heads, attended_heads, preferred_element_type=jnp.float32
    )[..., None]
    dscores = (prob * (dprob - delta) * scale).astype(jnp.bfloat16)
    dqueries = jnp.einsum(
        "bhqk,bkhe->bqhe", dscores, key_heads, preferred_element_type=jnp.float32
    ).reshape(tokens, local_width)
    dkeys = jnp.einsum(
        "bhqk,bqhe->bkhe", dscores, query_heads, preferred_element_type=jnp.float32
    ).reshape(tokens, local_width)
    dvalues = jnp.einsum(
        "bhqk,bqhe->bkhe", again_weights, dattended_heads, preferred_element_type=jnp.float32
    ).reshape(tokens, local_width)
    grad_bias_part = jnp.stack([jnp.sum(dqueries, axis=0), jnp.sum(dvalues, axis=0)])
    stacked = jnp.stack([dqueries, dkeys, dvalues]).astype(jnp.bfloat16)
    grad_qkv = jnp.einsum("rd,cre->cde", hidden_one, stacked, preferred_element_type=jnp.float32)
    dhidden_one = lax.psum(
        jnp.einsum("cre,cde->rd", stacked, back_qkv, preferred_element_type=jnp.float32).astype(
            jnp.bfloat16
        ),
        "tensor",
    ).astype(jnp.float32)
    grad_input = dmiddle + normalize_back(dhidden_one, normed_one, inverse_one, gain_rows[0])
    grad_gains = jnp.stack(
        [jnp.sum(dhidden_one * normed_one, axis=0), jnp.sum(dhidden_two * normed_two, axis=0)]
    )
    grad_shifts = jnp.stack([jnp.sum(dhidden_one, axis=0), jnp.sum(dhidden_two, axis=0)])
    owned_qkv, owned_out, owned_up, owned_down, owned_gains, owned_shifts, owned_bias = (
        lax.psum_scatter(
            grad_qkv.astype(jnp.bfloat16), "fsdp", scatter_dimension=1, tiled=True
        ).astype(jnp.float32),
        lax.psum_scatter(
            grad_out.astype(jnp.bfloat16), "fsdp", scatter_dimension=1, tiled=True
        ).astype(jnp.float32),
        lax.psum_scatter(
            grad_up.astype(jnp.bfloat16), "fsdp", scatter_dimension=0, tiled=True
        ).astype(jnp.float32),
        lax.psum_scatter(
            grad_down.astype(jnp.bfloat16), "fsdp", scatter_dimension=1, tiled=True
        ).astype(jnp.float32),
        lax.psum_scatter(
            grad_gains.astype(jnp.bfloat16), "fsdp", scatter_dimension=1, tiled=True
        ).astype(jnp.float32),
        lax.psum_scatter(
            grad_shifts.astype(jnp.bfloat16), "fsdp", scatter_dimension=1, tiled=True
        ).astype(jnp.float32),
        lax.psum_scatter(
            grad_out_bias.astype(jnp.bfloat16), "fsdp", scatter_dimension=1, tiled=True
        ).astype(jnp.float32),
    )
    summed_bias_qv, summed_b_up = lax.psum((grad_bias_part, grad_b_up), "fsdp")
    return (
        result.reshape(batch, seq_len, width),
        grad_input.reshape(batch, seq_len, width),
        owned_gains,
        owned_shifts,
        owned_qkv,
        summed_bias_qv,
        owned_out,
        owned_bias,
        owned_up,
        summed_b_up,
        owned_down,
    )


def solution(mesh):
    placed = (
        P("fsdp", None, None),
        P("fsdp"),
        P(None, "fsdp"),
        P(None, "fsdp"),
        P(None, "fsdp", "tensor"),
        P(None, "tensor"),
        P("tensor", "fsdp"),
        P(None, "fsdp"),
        P("fsdp", "tensor"),
        P("tensor"),
        P("tensor", "fsdp"),
        P("fsdp", None, None),
    )
    return jax.shard_map(
        local,
        mesh=mesh,
        in_specs=placed,
        out_specs=(
            P("fsdp", None, None),
            P("fsdp", None, None),
            P(None, "fsdp"),
            P(None, "fsdp"),
            P(None, "fsdp", "tensor"),
            P(None, "tensor"),
            P("tensor", "fsdp"),
            P(None, "fsdp"),
            P("fsdp", "tensor"),
            P("tensor"),
            P("tensor", "fsdp"),
        ),
        check_vma=False,
    )
```

profile of v0, /device:TPU:0, one launch (start us, length us, event | category | flops | bytes accessed | tf_op | source)
XLA Modules:
  0.0 1187.7 jit_solution(13304505593827600482)
XLA Ops:
  33.3 10.2 all_gather.21
  52.3 9.5 all_gather.24
  99.1 10.7 fusion.1
  109.8 11.2 exponential_reduce_fusion
  121.1 10.8 convolution_convert_fusion.7
  161.2 150.4 %all-reduce.6.cloned.1.call-done = bf16[2308,1024]{1,0:T(8,128)(2,1)} async-done(((bf16[2308,1024]{1,0:T(8,128)(2,1)}), bf16[2308,1024]{1,0:T(8,128)(2,1)}) %all-reduce.6.cloned.1.call-update) | async-done | bytes 4726800 | tf_op jit(solution)/shard_map/psum | solution.py:91
  311.6 10.0 fusion.66
  326.4 13.9 %all-gather.6.cloned.1.call-done = bf16[1024,1024]{1,0:T(8,128)(2,1)} async-done(((bf16[128,1024]{1,0:T(8,128)(2,1)}), bf16[1024,1024]{1,0:T(8,128)(2,1)}) %all-gather.6.cloned.1.call-update) | async-done | bytes 2097168 | tf_op jit(solution)/shard_map/all_gather | solution.py:59
  340.3 30.0 %fusion.20 = (bf16[2308,1024]{1,0:T(8,128)(2,1)}, f32[2308,1024]{1,0:T(8,128)}) fusion(f32[1024]{0:T(1024)S(1)} %convert_element_type.159, bf16[1024,1024]{1,0:T(8,128)(2,1)} %all-gather.6.cloned.1.call-done, f32[2308,1024]{1,0:T(8,128)} %get-tuple-element.70, f32[1024]{0:T(1024)S(1)} %bitcast.111, f32[1024]{0:T(1024)S(1)} %bitcast.100, ...), kind=kOutput, calls=%fused_computation.30 | convolution fusion | flops 5008027648 | bytes 25761824 | tf_op jit(solution)/shard_map/dot_general | solution.py:98
  370.3 12.2 %fusion.71 = (f32[1024]{0:T(1024)}, bf16[2308,1024]{1,0:T(8,128)(2,1)S(1)}) fusion(f32[2308,1024]{1,0:T(8,128)} %get-tuple-element.82, f32[1024]{0:T(1024)S(1)} %convert_element_type.159, bf16[2308,1024]{1,0:T(8,128)(2,1)} %reshape.151, bf16[1024,1024]{1,0:T(8,128)(2,1)} %all-gather.8.cloned.1.call-done), kind=kOutput, calls=%fused_computation.127 | convolution fusion | flops 4868586496 | bytes 21012480 | tf_op jit(solution)/shard_map/rd,fd->rf/dot_general | solution.py:109
  391.6 9.3 convolution_convert_fusion.4
  407.9 13.2 %fusion.40 = bf16[1024,1024]{1,0:T(8,128)(2,1)} fusion(bf16[2308,1024]{1,0:T(8,128)(2,1)} %copy-done.39, f32[2308,1024]{1,0:T(8,128)} %get-tuple-element.70, f32[1024]{0:T(1024)S(1)} %bitcast.112, f32[1024]{0:T(1024)S(1)} %bitcast.101, f32[2308]{0:T(1024)S(1)} %add_rsqrt_fusion.1, f32[2308]{0:T(1024)S(1)} %broadcast_multiply_fusion.5), kind=kOutput, calls=%fused_computation.81 | convolution fusion | flops 4853092352 | bytes 16304160 | tf_op jit(solution)/shard_map/rd,rf->df/dot_general | solution.py:115
  421.1 143.2 %all-reduce.8.cloned.1.call-done = bf16[2308,1024]{1,0:T(8,128)(2,1)} async-done(((bf16[2308,1024]{1,0:T(8,128)(2,1)}), bf16[2308,1024]{1,0:T(8,128)(2,1)}) %all-reduce.8.cloned.1.call-update) | async-done | bytes 4726800 | tf_op jit(solution)/shard_map/psum | solution.py:116
  564.4 9.2 fusion.12
  593.1 17.2 %multiply_convert_fusion = bf16[4,4,577,577]{2,3,1,0:T(8,128)(2,1)} fusion(f32[4,4,577,577]{2,3,1,0:T(8,128)} %get-tuple-element.80, f32[4,4,577]{2,1,0:T(4,128)S(1)} %multiply_reduce_fusion.2, f32[4,4,577]{2,1,0:T(4,128)S(1)} %bitcast.94, pred[4,577]{1,0:T(4,128)(4,1)S(1)} %copy-done.21, bf16[4,577,4,64]{1,0,3,2:T(4,128)(2,1)} %reshape.152, ...), kind=kOutput, calls=%fused_computation | convolution fusion | flops 719126592 | bytes 34400740 | tf_op jit(solution)/shard_map/bqhe,bkhe->bhqk/dot_general | solution.py:133
  627.9 9.6 fusion.44
  637.5 12.5 %bitcast_convert_fusion.1 = (bf16[4,577,4,64]{1,3,2,0:T(8,128)(2,1)}, f32[4,4,64,577]{3,2,1,0:T(8,128)}) fusion(f32[4,4,577,577]{2,3,1,0:T(8,128)} %get-tuple-element.80, f32[4,4,577]{2,1,0:T(4,128)S(1)} %bitcast.95, pred[4,577]{1,0:T(4,128)(4,1)S(1)} %copy-done.21, bf16[4,577,4,64]{1,0,3,2:T(4,128)(2,1)S(1)} %copy-done.11), kind=kOutput, calls=%fused_computation.68 | convolution fusion | flops 703736896 | bytes 26073476 | tf_op jit(solution)/shard_map/bhqk,bqhe->bkhe/dot_general | solution.py:146
  665.8 10.9 fusion.43
  681.5 9.5 convolution_convert_fusion.1
  706.2 13.9 %all-reduce = (f32[2,256]{1,0:T(2,128)}, f32[1024]{0:T(1024)}) all-reduce(f32[2,256]{1,0:T(2,128)S(1)} %pad_maximum_fusion.3, f32[1024]{0:T(1024)S(1)} %copy-done.29), channel_id=1, replica_groups=mesh['fsdp'=8,'tensor'=4] {'fsdp'}, use_global_device_ids=true, to_apply=%region_23.24 | all-reduce | flops 1536 | bytes 12288 | tf_op jit(solution)/shard_map/psum | solution.py:186
  728.3 39.9 %reduce-scatter.26.cloned.1.call-done = bf16[128,768]{1,0:T(8,128)(2,1)} async-done(((bf16[1024,768]{1,0:T(8,128)(2,1)}), bf16[128,768]{1,0:T(8,128)(2,1)}) %reduce-scatter.26.cloned.1.call-update) | async-done | bytes 196624
  770.3 327.2 %all-reduce.10.cloned.1.call-done = (bf16[2308,1024]{1,0:T(8,128)(2,1)}, bf16[2308,1024]{1,0:T(8,128)(2,1)}) async-done(((bf16[2308,1024]{1,0:T(8,128)(2,1)}, bf16[2308,1024]{1,0:T(8,128)(2,1)}), (bf16[2308,1024]{1,0:T(8,128)(2,1)}, bf16[2308,1024]{1,0:T(8,128)(2,1)})) %all-reduce.10.cloned.1.call-update) | async-done | bytes 9453584 | tf_op jit(solution)/shard_map/psum | solution.py:100
  1110.1 13.2 %fusion.15 = f32[2308,1024]{1,0:T(8,128)} fusion(f32[2308,1024]{1,0:T(8,128)} %copy-done, bf16[2308,1024]{1,0:T(8,128)(2,1)} %get-tuple-element.66, f32[2308,1024]{1,0:T(8,128)} %reshape.154, f32[2308]{0:T(1024)S(1)} %broadcast_multiply_fusion.1, f32[2308]{0:T(1024)S(1)} %broadcast_multiply_fusion.2, f32[1024]{0:T(1024)S(1)} %bitcast.99, ...), kind=kLoop, calls=%fused_computation.25 | loop fusion | flops 21270528 | bytes 33128512 | tf_op jit(solution)/shard_map/add | solution.py:158
  1155.7 13.8 %copy.130 = f32[4,577,1024]{2,0,1:T(4,128)} copy(f32[4,577,1024]{2,1,0:T(8,128)} %reshape.153) | data formatting | bytes 18907136
  (225 shorter events, 261.3 us)
Async XLA Ops:
  7.2 54.8 %all-gather.4.cloned.1.call-start = ((), (), s32[]{:S(2)}) async-start(), calls=%async_computation.7 | async-start | bytes 1769472 | tf_op jit(solution)/shard_map/all_gather | solution.py:57
  7.9 303.7 %all-reduce.6.cloned.1.call-start = ((), (), s32[]{:S(2)}) async-start(), calls=%async_computation.8 | async-start | bytes 9469952 | tf_op jit(solution)/shard_map/psum | solution.py:91
  24.8 37.1 %copy-start.16 = (f32[2308]{0:T(1024)}, f32[2308]{0:T(1024)S(1)}, u32[]{:S(2)}) copy-start(f32[2308]{0:T(1024)S(1)} %rsqrt.20) | copy-start | bytes 27700
  24.9 37.1 %copy-start.18 = (f32[2308]{0:T(1024)}, f32[2308]{0:T(1024)S(1)}, u32[]{:S(2)}) copy-start(f32[2308]{0:T(1024)S(1)} %div.27) | copy-start | bytes 27700
  24.9 27.4 %copy-start.22 = (bf16[256,128]{1,0:T(8,128)(2,1)S(1)}, bf16[256,128]{1,0:T(8,128)(2,1)}, u32[]{:S(2)}) copy-start(bf16[256,128]{1,0:T(8,128)(2,1)} %param.18) | copy-start | bytes 196612
  24.9 36.9 %copy-start.36 = (s32[4]{0:T(128)S(1)}, s32[4]{0:T(128)}, u32[]{:S(2)}) copy-start(s32[4]{0:T(128)} %param.13) | copy-start | bytes 52
  61.8 73.2 %copy-start.12 = (bf16[256,1024]{1,0:T(8,128)(2,1)}, bf16[256,1024]{1,0:T(8,128)(2,1)S(1)}, u32[]{:S(2)}) copy-start(bf16[256,1024]{1,0:T(8,128)(2,1)S(1)} %all_gather.24) | copy-start | bytes 1572868
  61.9 59.2 %copy-start.20 = (pred[4,577]{1,0:T(4,128)(4,1)}, pred[4,577]{1,0:T(4,128)(4,1)S(1)}, u32[]{:S(2)}) copy-start(pred[4,577]{1,0:T(4,128)(4,1)S(1)} %iota_compare_fusion) | copy-start | bytes 6928
  86.2 23.6 %copy-start.6 = (bf16[4,577,4,64]{1,3,2,0:T(8,128)(2,1)}, bf16[4,577,4,64]{1,3,2,0:T(8,128)(2,1)S(1)}, u32[]{:S(2)}) copy-start(bf16[4,577,4,64]{1,3,2,0:T(8,128)(2,1)S(1)} %copy.108) | copy-start | bytes 3545092
  99.1 22.0 %copy-start.14 = (bf16[4,577,4,64]{1,0,3,2:T(4,128)(2,1)}, bf16[4,577,4,64]{1,0,3,2:T(4,128)(2,1)S(1)}, u32[]{:S(2)}) copy-start(bf16[4,577,4,64]{1,0,3,2:T(4,128)(2,1)S(1)} %add_convert_fusion.4) | copy-start | bytes 3545092
  135.0 20.4 %copy-start.4 = (bf16[2308,256]{0,1:T(8,128)(2,1)}, bf16[2308,256]{0,1:T(8,128)(2,1)S(1)}, u32[]{:S(2)}) copy-start(bf16[2308,256]{0,1:T(8,128)(2,1)S(1)} %reshape.149) | copy-start | bytes 3545092
  138.5 201.7 %all-gather.6.cloned.1.call-start = ((), (), s32[]{:S(2)}) async-start(), calls=%async_computation.9 | async-start | bytes 2359296 | tf_op jit(solution)/shard_map/all_gather | solution.py:59
  139.3 231.0 %all-gather.8.cloned.1.call-start = ((), (), s32[]{:S(2)}) async-start(), calls=%async_computation.10 | async-start | bytes 2359296 | tf_op jit(solution)/shard_map/all_gather | solution.py:60
  139.9 424.5 %all-reduce.8.cloned.1.call-start = ((), (), s32[]{:S(2)}) async-start(), calls=%async_computation.11 | async-start | bytes 9469952 | tf_op jit(solution)/shard_map/psum | solution.py:116
  391.5 305.1 %reduce-scatter.32.cloned.1.call-start = ((), (), s32[]{:S(2)}) async-start(), calls=%async_computation.18 | async-start | bytes 2359296
  403.6 295.2 %reduce-scatter.20.cloned.1.call-start = ((), (), s32[]{:S(2)}) async-start(), calls=%async_computation.12 | async-start | bytes 2359296 | tf_op jit(solution)/shard_map/reduce_scatter | solution.py:170
  421.1 298.9 %reduce-scatter.30.cloned.1.call-start = ((), (), s32[]{:S(2)}) async-start(), calls=%async_computation.17 | async-start | bytes 294912
  650.0 76.7 %reduce-scatter.28.cloned.1.call-start = ((), (), s32[]{:S(2)}) async-start(), calls=%async_computation.16 | async-start | bytes 589824
  662.3 105.9 %reduce-scatter.26.cloned.1.call-start = ((), (), s32[]{:S(2)}) async-start(), calls=%async_computation.15 | async-start | bytes 1769472
  681.4 416.1 %all-reduce.10.cloned.1.call-start = ((), (), s32[]{:S(2)}) async-start(), calls=%async_computation.19 | async-start | bytes 18939904 | tf_op jit(solution)/shard_map/psum | solution.py:100
  696.6 404.0 %copy-start.17 = (f32[2308]{0:T(1024)S(1)}, f32[2308]{0:T(1024)}, u32[]{:S(2)}) copy-start(f32[2308]{0:T(1024)} %copy-done.16) | copy-start | bytes 27700
  696.6 404.0 %copy-start.19 = (f32[2308]{0:T(1024)S(1)}, f32[2308]{0:T(1024)}, u32[]{:S(2)}) copy-start(f32[2308]{0:T(1024)} %copy-done.18) | copy-start | bytes 27700
  696.6 472.9 %reduce-scatter.22.cloned.1.call-start = ((), (), s32[]{:S(2)}) async-start(), calls=%async_computation.13 | async-start | bytes 294912
  1110.0 69.5 %reduce-scatter.24.cloned.1.call-start = ((), (), s32[]{:S(2)}) async-start(), calls=%async_computation.14 | async-start | bytes 294912
  (31 other events, 295.5 us)
Sparse Core Ops, SparseCore 0:
  9.9 28.2 all-gather.3
  138.7 172.9 all-reduce.5
  313.5 26.7 all-gather.5
  342.0 28.0 all-gather.7
  391.7 172.6 all-reduce.7
  567.5 40.0 reduce-scatter.31
  610.9 41.1 reduce-scatter.19
  655.6 33.7 reduce-scatter.29
  692.5 34.2 reduce-scatter.27
  729.9 38.3 reduce-scatter.25
  771.4 326.0 all-reduce.9
  1110.1 32.6 reduce-scatter.21
  1145.8 33.6 reduce-scatter.23
where the time goes:
time: 1200 us; the launch traced here: 1190 us
  waiting for transfers between devices  691 us (58%)
  matrix products  182 us (15%)
  local copies, waits for them, and re-layouts  142 us (12%)
  other arithmetic  107 us (9%)
  blocking collectives  51.1 us (4%)
  between operations  14.9 us (1%)
    psum x1, waiting for transfers between devices, local(): lax.psum(jnp.dot(activated, full_down, preferred_element_type=jnp.float32...  327 us
    psum x1, waiting for transfers between devices, local(): lax.psum(jnp.dot(attended, full_out, preferred_element_type=jnp.float32)....  150 us
    psum x1, waiting for transfers between devices, local(): lax.psum(jnp.einsum('rf,df->rd', dbefore_b, back_up, preferred_element_ty...  143 us
    unnamed x19, waiting for transfers between devices  55.8 us
    unnamed x106, local copies, waits for them, and re-layouts  53.4 us
    dot_general x1, matrix products, local(): jnp.dot(hidden_two, full_up, preferred_element_type=jnp.float32)  30 us
  transfers between devices with their start and end apart: 13, of which 7 were waited for; matrix products, arithmetic and copies ran while one was open for 27% of the time, Pallas kernels for 0%

commit v1 on v0

--- a/solution.py
+++ b/solution.py
@@ -97,9 +97,12 @@
     hidden_two = (normed_two * gain_rows[1] + shift_rows[1]).astype(jnp.bfloat16)
     before = jnp.dot(hidden_two, full_up, preferred_element_type=jnp.float32) + hidden_bias
     activated = jax.nn.gelu(before, approximate=False).astype(jnp.bfloat16)
-    mlp_total = lax.psum(
-        jnp.dot(activated, full_down, preferred_element_type=jnp.float32).astype(jnp.bfloat16),
-        "tensor",
+    mlp_total = jnp.sum(
+        lax.all_gather(
+            jnp.dot(activated, full_down, preferred_element_type=jnp.float32).astype(jnp.bfloat16),
+            "tensor",
+        ),
+        axis=0,
     ).astype(jnp.float32)
     result = (middle + (mlp_total + bias_rows[1])).astype(jnp.bfloat16)
     back_qkv, back_out, back_up, back_down = (full_qkv, full_out, full_up, full_down)

time: 1200 us -> 1370 us (1.14)
  waiting for transfers between devices: 691 us -> 851 us
    all_gather x0 -> x1, waiting for transfers between devices: none -> 316 us  [local(): lax.all_gather(jnp.dot(activated, full_down, preferred_element_type=jnp.f...]
    psum x1, waiting for transfers between devices: 327 us -> 173 us  [local(): lax.psum(jnp.einsum('cre,cde->rd', stacked, back_qkv, preferred_element_t...]
    reduce_sum x0 -> x1, other arithmetic: none -> 16.7 us  [local(): jnp.sum(lax.all_gather(jnp.dot(activated, full_down, preferred_element_ty...]
    unnamed x19 -> x20, waiting for transfers between devices: 55.8 us -> 64.6 us
    unnamed x106 -> x98, local copies, waits for them, and re-layouts: 53.4 us -> 53.1 us
  transfers between devices with their start and end apart: 13 -> 14, of which waited for: 7 -> 7; matrix products, arithmetic and copies ran while one was open for 27% -> 24% of each run, Pallas kernels for 0% -> 0%
where the time goes in v1:
time: 1370 us; the launch traced here: 1360 us
  waiting for transfers between devices  851 us (62%)
  matrix products  184 us (13%)
  local copies, waits for them, and re-layouts  141 us (10%)
  other arithmetic  119 us (9%)
  blocking collectives  51.8 us (4%)
  between operations  14.8 us (1%)
    all_gather x1, waiting for transfers between devices, local(): lax.all_gather(jnp.dot(activated, full_down, preferred_element_type=jnp.f...  316 us
    psum x1, waiting for transfers between devices, local(): lax.psum(jnp.einsum('cre,cde->rd', stacked, back_qkv, preferred_element_t...  173 us
    psum x1, waiting for transfers between devices, local(): lax.psum(jnp.dot(attended, full_out, preferred_element_type=jnp.float32)....  150 us
    psum x1, waiting for transfers between devices, local(): lax.psum(jnp.einsum('rf,df->rd', dbefore_b, back_up, preferred_element_ty...  134 us
    unnamed x20, waiting for transfers between devices  64.6 us
    unnamed x98, local copies, waits for them, and re-layouts  53.1 us
    dot_general x1, matrix products, local(): jnp.dot(hidden_two, full_up, preferred_element_type=jnp.float32)  30 us
  transfers between devices with their start and end apart: 14, of which 7 were waited for; matrix products, arithmetic and copies ran while one was open for 24% of the time, Pallas kernels for 0%

profile of v1, /device:TPU:0, one launch (start us, length us, event | category | flops | bytes accessed | tf_op | source)
XLA Modules:
  0.0 1362.6 jit_solution(15563754438792900226)
XLA Ops:
  33.4 10.2 all_gather.27
  99.1 10.7 fusion.1
  109.8 11.2 exponential_reduce_fusion
  121.0 10.8 convolution_convert_fusion.7
  161.1 150.5 %all-reduce.5.cloned.1.call-done = bf16[2308,1024]{1,0:T(8,128)(2,1)} async-done(((bf16[2308,1024]{1,0:T(8,128)(2,1)}), bf16[2308,1024]{1,0:T(8,128)(2,1)}) %all-reduce.5.cloned.1.call-update) | async-done | bytes 4726800 | tf_op jit(solution)/shard_map/psum | solution.py:91
  311.6 10.1 fusion.67
  326.5 13.8 %all-gather.9.cloned.1.call-done = bf16[1024,1024]{1,0:T(8,128)(2,1)} async-done(((bf16[128,1024]{1,0:T(8,128)(2,1)}), bf16[1024,1024]{1,0:T(8,128)(2,1)}) %all-gather.9.cloned.1.call-update) | async-done | bytes 2097168 | tf_op jit(solution)/shard_map/all_gather | solution.py:59
  340.3 30.0 %fusion.20 = (bf16[2308,1024]{1,0:T(8,128)(2,1)}, f32[2308,1024]{1,0:T(8,128)}) fusion(f32[1024]{0:T(1024)S(1)} %convert_element_type.161, bf16[1024,1024]{1,0:T(8,128)(2,1)} %all-gather.9.cloned.1.call-done, f32[2308,1024]{1,0:T(8,128)} %get-tuple-element.68, f32[1024]{0:T(1024)S(1)} %bitcast.113, f32[1024]{0:T(1024)S(1)} %bitcast.102, ...), kind=kOutput, calls=%fused_computation.30 | convolution fusion | flops 5008027648 | bytes 25761824 | tf_op jit(solution)/shard_map/dot_general | solution.py:98
  370.3 12.2 fusion.72
  391.7 9.5 fusion.33
  417.2 13.2 fusion.41
  430.7 133.8 %all-reduce.7.cloned.1.call-done = bf16[2308,1024]{1,0:T(8,128)(2,1)} async-done(((bf16[2308,1024]{1,0:T(8,128)(2,1)}), bf16[2308,1024]{1,0:T(8,128)(2,1)}) %all-reduce.7.cloned.1.call-update) | async-done | bytes 4726800 | tf_op jit(solution)/shard_map/psum | solution.py:119
  572.8 315.7 %all-gather.13.cloned.1.call-done = bf16[4,2308,1024]{2,1,0:T(8,128)(2,1)} async-done(((bf16[1,2308,1024]{2,1,0:T(8,128)(2,1)}), bf16[4,2308,1024]{2,1,0:T(8,128)(2,1)}) %all-gather.13.cloned.1.call-update) | async-done | bytes 18907152 | tf_op jit(solution)/shard_map/all_gather | solution.py:101
  888.5 16.7 %reduce_sum.179 = bf16[2308,1024]{1,0:T(8,128)(2,1)} reduce(bf16[4,2308,1024]{2,1,0:T(8,128)(2,1)} %all-gather.13.cloned.1.call-done, bf16[]{:T(256)} %constant.80.clone.1), dimensions={0}, to_apply=%region_7.8 | reduce | flops 7090176 | bytes 23633922 | tf_op jit(solution)/shard_map/reduce_sum | solution.py:100
  905.3 12.5 fusion.65
  929.3 17.2 %multiply_convert_fusion = bf16[4,4,577,577]{2,3,1,0:T(8,128)(2,1)} fusion(f32[4,4,577,577]{2,3,1,0:T(8,128)} %get-tuple-element.79, f32[4,4,577]{2,1,0:T(4,128)S(1)} %multiply_reduce_fusion.2, f32[4,4,577]{2,1,0:T(4,128)S(1)} %bitcast.96, pred[4,577]{1,0:T(4,128)(4,1)S(1)} %copy-done.19, bf16[4,577,4,64]{1,0,3,2:T(4,128)(2,1)} %reshape.152, ...), kind=kOutput, calls=%fused_computation | convolution fusion | flops 719126592 | bytes 34400740 | tf_op jit(solution)/shard_map/bqhe,bkhe->bhqk/dot_general | solution.py:136
  973.4 12.4 bitcast_convert_fusion.1
  1001.7 10.9 fusion.44
  1049.5 14.6 %all-reduce = (f32[2,256]{1,0:T(2,128)}, f32[1024]{0:T(1024)}) all-reduce(f32[2,256]{1,0:T(2,128)S(1)} %pad_maximum_fusion.3, f32[1024]{0:T(1024)S(1)} %copy-done.26), channel_id=1, replica_groups=mesh['fsdp'=8,'tensor'=4] {'fsdp'}, use_global_device_ids=true, to_apply=%region_23.24 | all-reduce | flops 1536 | bytes 12288 | tf_op jit(solution)/shard_map/psum | solution.py:189
  1067.2 30.4 %reduce-scatter.26.cloned.1.call-done = bf16[128,768]{1,0:T(8,128)(2,1)} async-done(((bf16[1024,768]{1,0:T(8,128)(2,1)}), bf16[128,768]{1,0:T(8,128)(2,1)}) %reduce-scatter.26.cloned.1.call-update) | async-done | bytes 196624
  1099.7 172.8 %all-reduce.9.cloned.1.call-done = bf16[2308,1024]{1,0:T(8,128)(2,1)} async-done(((bf16[2308,1024]{1,0:T(8,128)(2,1)}), bf16[2308,1024]{1,0:T(8,128)(2,1)}) %all-reduce.9.cloned.1.call-update) | async-done | bytes 4726800 | tf_op jit(solution)/shard_map/psum | solution.py:155
  1285.9 13.0 fusion.15
  1307.4 13.6 copy.130
  1322.3 32.1 %reduce-scatter.24.cloned.1.call-done = bf16[128,2]{1,0:T(8,128)(2,1)} async-done(((bf16[1024,2]{1,0:T(8,128)(2,1)}), bf16[128,2]{1,0:T(8,128)(2,1)}) %reduce-scatter.24.cloned.1.call-update) | async-done | bytes 528
  (220 shorter events, 270.0 us)
Async XLA Ops:
  7.2 54.7 %all-gather.7.cloned.1.call-start = ((), (), s32[]{:S(2)}) async-start(), calls=%async_computation.7 | async-start | bytes 1769472 | tf_op jit(solution)/shard_map/all_gather | solution.py:57
  7.9 303.7 %all-reduce.5.cloned.1.call-start = ((), (), s32[]{:S(2)}) async-start(), calls=%async_computation.8 | async-start | bytes 9469952 | tf_op jit(solution)/shard_map/psum | solution.py:91
  24.8 37.1 %copy-start.14 = (f32[2308]{0:T(1024)}, f32[2308]{0:T(1024)S(1)}, u32[]{:S(2)}) copy-start(f32[2308]{0:T(1024)S(1)} %rsqrt.20) | copy-start | bytes 27700
  24.9 37.0 %copy-start.16 = (f32[2308]{0:T(1024)}, f32[2308]{0:T(1024)S(1)}, u32[]{:S(2)}) copy-start(f32[2308]{0:T(1024)S(1)} %div.27) | copy-start | bytes 27700
  24.9 27.4 %copy-start.20 = (bf16[256,128]{1,0:T(8,128)(2,1)S(1)}, bf16[256,128]{1,0:T(8,128)(2,1)}, u32[]{:S(2)}) copy-start(bf16[256,128]{1,0:T(8,128)(2,1)} %param.18) | copy-start | bytes 196612
  24.9 36.8 %copy-start.32 = (s32[4]{0:T(128)S(1)}, s32[4]{0:T(128)}, u32[]{:S(2)}) copy-start(s32[4]{0:T(128)} %param.13) | copy-start | bytes 52
  61.7 73.2 %copy-start.11 = (bf16[256,1024]{1,0:T(8,128)(2,1)}, bf16[256,1024]{1,0:T(8,128)(2,1)S(1)}, u32[]{:S(2)}) copy-start(bf16[256,1024]{1,0:T(8,128)(2,1)S(1)} %all_gather.30) | copy-start | bytes 1572868
  61.8 59.2 %copy-start.18 = (pred[4,577]{1,0:T(4,128)(4,1)}, pred[4,577]{1,0:T(4,128)(4,1)S(1)}, u32[]{:S(2)}) copy-start(pred[4,577]{1,0:T(4,128)(4,1)S(1)} %iota_compare_fusion) | copy-start | bytes 6928
  86.1 23.6 %copy-start.5 = (bf16[4,577,4,64]{1,3,2,0:T(8,128)(2,1)}, bf16[4,577,4,64]{1,3,2,0:T(8,128)(2,1)S(1)}, u32[]{:S(2)}) copy-start(bf16[4,577,4,64]{1,3,2,0:T(8,128)(2,1)S(1)} %copy.108) | copy-start | bytes 3545092
  138.5 201.7 %all-gather.9.cloned.1.call-start = ((), (), s32[]{:S(2)}) async-start(), calls=%async_computation.9 | async-start | bytes 2359296 | tf_op jit(solution)/shard_map/all_gather | solution.py:59
  139.3 231.0 %all-gather.11.cloned.1.call-start = ((), (), s32[]{:S(2)}) async-start(), calls=%async_computation.10 | async-start | bytes 2359296 | tf_op jit(solution)/shard_map/all_gather | solution.py:60
  139.8 424.6 %all-reduce.7.cloned.1.call-start = ((), (), s32[]{:S(2)}) async-start(), calls=%async_computation.11 | async-start | bytes 9469952 | tf_op jit(solution)/shard_map/psum | solution.py:119
  391.6 496.9 %all-gather.13.cloned.1.call-start = ((), (), s32[]{:S(2)}) async-start(), calls=%async_computation.14 | async-start | bytes 23674880 | tf_op jit(solution)/shard_map/all_gather | solution.py:101
  401.3 624.7 %reduce-scatter.32.cloned.1.call-start = ((), (), s32[]{:S(2)}) async-start(), calls=%async_computation.20 | async-start | bytes 2359296
  412.9 615.2 %reduce-scatter.20.cloned.1.call-start = ((), (), s32[]{:S(2)}) async-start(), calls=%async_computation.13 | async-start | bytes 2359296 | tf_op jit(solution)/shard_map/reduce_scatter | solution.py:173
  430.4 633.7 %reduce-scatter.30.cloned.1.call-start = ((), (), s32[]{:S(2)}) async-start(), calls=%async_computation.19 | async-start | bytes 294912
  572.8 332.5 %copy-start.25 = (f32[1,1024]{1,0:T(1,128)S(1)}, f32[1,1024]{1,0:T(1,128)}, u32[]{:S(2)}) copy-start(f32[1,1024]{1,0:T(1,128)} %get-tuple-element.72) | copy-start | bytes 12292
  985.8 79.7 %reduce-scatter.28.cloned.1.call-start = ((), (), s32[]{:S(2)}) async-start(), calls=%async_computation.18 | async-start | bytes 589824
  998.2 99.4 %reduce-scatter.26.cloned.1.call-start = ((), (), s32[]{:S(2)}) async-start(), calls=%async_computation.17 | async-start | bytes 1769472
  1017.1 255.4 %all-reduce.9.cloned.1.call-start = ((), (), s32[]{:S(2)}) async-start(), calls=%async_computation.12 | async-start | bytes 9469952 | tf_op jit(solution)/shard_map/psum | solution.py:155
  1025.9 295.0 %reduce-scatter.22.cloned.1.call-start = ((), (), s32[]{:S(2)}) async-start(), calls=%async_computation.15 | async-start | bytes 294912
  1041.2 234.4 %copy-start.15 = (f32[2308]{0:T(1024)S(1)}, f32[2308]{0:T(1024)}, u32[]{:S(2)}) copy-start(f32[2308]{0:T(1024)} %copy-done.14) | copy-start | bytes 27700
  1041.2 234.4 %copy-start.17 = (f32[2308]{0:T(1024)S(1)}, f32[2308]{0:T(1024)}, u32[]{:S(2)}) copy-start(f32[2308]{0:T(1024)} %copy-done.16) | copy-start | bytes 27700
  1285.0 69.4 %reduce-scatter.24.cloned.1.call-start = ((), (), s32[]{:S(2)}) async-start(), calls=%async_computation.16 | async-start | bytes 294912
  (28 other events, 289.8 us)
Sparse Core Ops, SparseCore 0:
  9.9 28.2 all-gather.6
  138.6 172.8 all-reduce.4
  313.5 26.7 all-gather.8
  342.0 28.0 all-gather.10
  391.8 172.6 all-reduce.6
  565.9 322.5 all-gather.12
  891.8 39.9 reduce-scatter.31
  935.1 41.1 reduce-scatter.19
  986.0 32.8 reduce-scatter.29
  1021.8 34.0 reduce-scatter.27
  1059.2 38.3 reduce-scatter.25
  1099.8 172.6 all-reduce.8
  1285.1 32.6 reduce-scatter.21
  1320.7 33.7 reduce-scatter.23
